TPU v7x, 256 devices: a whole 4x4x8 slice. The times are simulated.
256 devices in a mesh: param: 16 (over x, y), space: 2 (over core), term: 8 (over z).
Axes of the slice: x: 4, y: 4, z: 8, core: 2. Of those that a mesh axis runs over, the one named last changes fastest.
Arguments:
- fields: float32 [128, 2, 8, 128, 128], P('param', None, None, 'space'), may hold values from -4 to 4
- library: int32 [168, 4], P('term'), may hold values from 0 to 6, as said below
- centers_x: int32 [16], replicated, may hold values from 0 to 127
- centers_y: int32 [16], replicated, may hold values from 0 to 127
- centers_t: int32 [4], replicated, may hold values from 0 to 7
- groups: int32 [168], replicated, may hold values from 0 to 23
Outputs:
- coefficients: float32 [128, 2, 168], P(('param', 'term'))
- misfit: float32 [128, 2, 168], P(('param', 'term'))
Inputs may be any that keep to these rules, and one draw needn't show every extreme that they name: `library`: each row (a, b, dx, dy) gives powers a and b of 0 to 6 and derivative orders dx and dy of 0 to 2; rows are distinct, and a = b = 0 only with dx = dy = 0.
All inputs are finite; a program needn't handle non-finite values.
Results may differ from a plain program's by a relative error of at most 0.00011.
Values sent between devices are 32-bit elements; how exact they have to be, the bound alone decides.
A program may use at most 64 MiB of HBM per device.

v0:
```python
import jax
import jax.numpy as jnp
from jax import lax
from jax.sharding import PartitionSpec as P

NX = 128
NY = 128
NT = 8
POWERS = 7
TERMS = 168
TESTS = 1024
RX = 16
RT = 4
GROUPS = 24


highest = lax.Precision.HIGHEST


def space_table(centers, first_row, row_count, extent):
    cell_index = first_row + jnp.arange(row_count, dtype=jnp.int32)
    offset = (cell_index[None, :] - centers[:, None] + extent // 2) % extent - extent // 2
    scaled = offset.astype(jnp.float32) / RX
    bump_base = 1.0 - scaled * scaled
    inside = jnp.abs(scaled) < 1.0
    cube = bump_base * bump_base * bump_base
    bump_value = jnp.where(inside, cube * bump_base, 0.0)
    bump_first = jnp.where(inside, 8.0 * scaled * cube / RX, 0.0)
    bump_second = jnp.where(
        inside, -8.0 * (cube - 6.0 * scaled * scaled * bump_base * bump_base) / (RX * RX), 0.0
    )
    return jnp.stack([bump_value, bump_first, bump_second])


def time_table(centers):
    step_index = jnp.arange(NT, dtype=jnp.int32)
    scaled = (step_index[None, :] - centers[:, None]).astype(jnp.float32) / RT
    bump_base = 1.0 - scaled * scaled
    inside = jnp.abs(scaled) < 1.0
    time_bump = jnp.where(inside, bump_base * bump_base, 0.0)
    time_slope = jnp.where(inside, 4.0 * scaled * bump_base / RT, 0.0)
    return (time_bump, time_slope)


def normalize(gram_matrix):
    diagonal = jnp.diagonal(gram_matrix, axis1=1, axis2=2)
    row_scale = jnp.sqrt(diagonal / TESTS + 1e-06)
    term_scale = row_scale[:, :TERMS]
    correlation = gram_matrix[:, :TERMS, :TERMS] / (
        TESTS * term_scale[:, :, None] * term_scale[:, None, :]
    )
    right_side = gram_matrix[:, TERMS:, :TERMS] / (
        TESTS * term_scale[:, None, :] * row_scale[:, TERMS:, None]
    )
    frobenius = jnp.sqrt(jnp.sum(correlation * correlation, axis=(1, 2)))
    return (correlation, right_side, frobenius)


def group_squares(values, onehot):
    return jnp.dot(jnp.sum(values * values, axis=(0, 1)), onehot, precision=highest)


def shrink(values, totals, onehot):
    threshold = 0.7 * jnp.sqrt(jnp.mean(totals))
    per_term = jnp.dot(onehot, totals, precision=highest)
    factor = jnp.maximum(0.0, 1.0 - threshold / jnp.sqrt(per_term + 1e-12))
    return values * factor


def correlate(correlation, values):
    return jnp.einsum("pij,psj->psi", correlation, values, precision=highest)


def body(fields, library, centers_x, centers_y, centers_t, groups):
    pgroup = fields.shape[0]
    tile_rows = fields.shape[3]
    space_count = lax.axis_size("space")
    term_count = lax.axis_size("term")
    local_terms = library.shape[0]
    row_count = local_terms + 2
    half_tests = TESTS // space_count
    y_table = space_table(centers_y, 0, NY, NY)
    time_bump, time_slope = time_table(centers_t)
    x_table = space_table(centers_x, lax.axis_index("space") * tile_rows, tile_rows, NX)
    share_rows = tile_rows // term_count
    share_start = lax.axis_index("term") * share_rows
    x_share = lax.dynamic_slice_in_dim(x_table[0], share_start, share_rows, 1)
    power_a = library[:, 0]
    power_b = library[:, 1]
    orders = jnp.arange(3, dtype=jnp.int32)
    pick_x = (library[:, 2][:, None] == orders[None, :]).astype(jnp.float32)
    pick_y = (library[:, 3][:, None] == orders[None, :]).astype(jnp.float32)
    x_pick = jnp.einsum("jd,dlx->jlx", pick_x, x_table, precision=highest)
    y_pick = jnp.einsum("jd,dky->jky", pick_y, y_table, precision=highest)

    def tile_integrals(field_pair):
        species_u = field_pair[0]
        species_v = field_pair[1]
        power_u = jnp.ones((local_terms,) + species_u.shape, jnp.float32)
        power_v = jnp.ones((local_terms,) + species_v.shape, jnp.float32)
        for degree in range(1, POWERS):
            power_u = power_u * jnp.where(
                power_a[:, None, None, None] >= degree, species_u[None], 1.0
            )
            power_v = power_v * jnp.where(
                power_b[:, None, None, None] >= degree, species_v[None], 1.0
            )
        monomial = power_u * power_v
        across_y = jnp.einsum("jtxy,jky->jtxk", monomial, y_pick, precision=highest)
        across_t = jnp.einsum("jtxk,rt->jrxk", across_y, time_bump, precision=highest)
        features = jnp.einsum("jrxk,jlx->jrkl", across_t, x_pick, precision=highest).reshape(
            local_terms, TESTS
        )
        share = lax.dynamic_slice_in_dim(field_pair, share_start, share_rows, 2)
        target_y = jnp.einsum("stxy,ky->stxk", share, y_table[0], precision=highest)
        targets = jnp.einsum(
            "stxk,rt,lx->srkl", target_y, time_slope, x_share, precision=highest
        ).reshape(2, TESTS)
        joined = jnp.concatenate([features, targets], axis=0).reshape(
            row_count, space_count, half_tests
        )
        return jnp.swapaxes(joined, 0, 1)

    def fill_param(index, buffer):
        field_pair = lax.dynamic_index_in_dim(fields, index, 0, keepdims=False)
        return lax.dynamic_update_slice_in_dim(
            buffer, tile_integrals(field_pair)[:, None], index, 1
        )

    buffer = jnp.zeros((space_count, pgroup, row_count, half_tests), jnp.float32)
    buffer = lax.fori_loop(0, pgroup, fill_param, buffer)
    received = lax.all_to_all(
        buffer.reshape(space_count * pgroup, row_count, half_tests),
        ("space", "term"),
        split_axis=0,
        concat_axis=1,
        tiled=True,
    )
    blocks = jnp.sum(received.reshape(space_count, term_count, row_count, half_tests), axis=0)
    features_half = blocks[:, :local_terms].reshape(term_count * local_terms, half_tests)
    targets_half = jnp.sum(blocks[:, local_terms:], axis=0)
    half_rows = jnp.concatenate([features_half, targets_half], axis=0)
    whole_rows = lax.all_gather(half_rows, "space", axis=1, tiled=True)
    gram_matrix = jnp.dot(whole_rows, whole_rows.T, precision=highest)[None]
    correlation, right_side, frobenius = normalize(gram_matrix)
    onehot = (groups[:, None] == jnp.arange(GROUPS, dtype=jnp.int32)[None, :]).astype(jnp.float32)
    largest = lax.pmax(jnp.max(frobenius), ("param", "term"))
    step_size = 1.0 / largest
    first_guess = step_size * right_side
    first_sq = lax.psum(group_squares(first_guess, onehot), ("param", "term"))
    first = shrink(first_guess, first_sq, onehot)
    second_guess = first - step_size * (correlate(correlation, first) - right_side)
    second_sq = lax.psum(group_squares(second_guess, onehot), ("param", "term"))
    second = shrink(second_guess, second_sq, onehot)
    coefficients = second / step_size
    misfit = right_side - correlate(correlation, second)
    return (coefficients, misfit)


def solution(mesh):
    return jax.shard_map(
        body,
        mesh=mesh,
        in_specs=(P("param", None, None, "space", None), P("term", None), P(), P(), P(), P()),
        out_specs=(P(("param", "term"), None, None), P(("param", "term"), None, None)),
        check_vma=False,
    )
```

profile of v0, /device:TPU:0, one launch (start us, length us, event | category | flops | bytes accessed | tf_op | source)
XLA Modules:
  0.0 1257.9 jit_solution(2309411352389409611)
XLA Ops:
  0.6 0.8 multiply_select_fusion.2
  1.5 0.7 fusion.127
  2.2 0.8 slice_bitcast_fusion.1
  3.4 0.8 multiply_select_fusion.5
  4.6 175.0 %while.18 = (s32[]{:T(128)}, f32[2,8,23,512]{3,0,2,1:T(2,128)S(1)}, s32[21,1]{0,1:T(1,128)S(1)}, f32[8,2,8,64,128]{4,3,2,1,0:T(8,128)}, s32[21,1]{0,1:T(1,128)S(...) while((s32[]{:T(128)}, f32[2,8,23,512]{3,0,2,1:T(2,128)S(1)}, ...), condition=%wide.region_1.2_spmd.clone.clone, body=%wide.region_0.1_spmd.clone.clone.sunk | while | flops 324181856 | bytes 4605749 | solution.py:131
  4.6 1.1 dynamic-slice_bitcast_fusion.6
  5.7 16.0 %fusion.203 = f32[21,8,64,16]{2,3,1,0:T(8,128)S(1)} fusion(f32[8,64,128]{2,1,0:T(8,128)S(1)} %get-tuple-element.566, f32[8,64,128]{2,1,0:T(8,128)S(1)} %get-tuple-element.567, pred[21]{0:T(512)(128)(4,1)S(1)} %get-tuple-element.568, pred[21]{0:T(512)(128)(4,1)S(1)} %get-tuple-element.569, pred[21]{0:T(512)(128)(4,1)S(1)} %get-tuple-element.570, ...), kind=kOutput, calls=%fused_computation.4.clone.1 | convolution fusion | flops 295895040 | bytes 1384700 | tf_op jit(solution)/shard_map/while/body/eval_jaxpr/jtxy,jky->jtxk/dot_general | solution.py:109
  21.7 1.6 fusion.204
  23.4 0.7 fusion.205
  24.1 0.4 concatenate.36
  24.5 0.9 dynamic-slice_bitcast_fusion.5
  26.5 1.1 dynamic-slice_bitcast_fusion.6
  27.6 16.0 %fusion.203 = f32[21,8,64,16]{2,3,1,0:T(8,128)S(1)} fusion(f32[8,64,128]{2,1,0:T(8,128)S(1)} %get-tuple-element.566, f32[8,64,128]{2,1,0:T(8,128)S(1)} %get-tuple-element.567, pred[21]{0:T(512)(128)(4,1)S(1)} %get-tuple-element.568, pred[21]{0:T(512)(128)(4,1)S(1)} %get-tuple-element.569, pred[21]{0:T(512)(128)(4,1)S(1)} %get-tuple-element.570, ...), kind=kOutput, calls=%fused_computation.4.clone.1 | convolution fusion | flops 295895040 | bytes 1384700 | tf_op jit(solution)/shard_map/while/body/eval_jaxpr/jtxy,jky->jtxk/dot_general | solution.py:109
  43.6 1.6 fusion.204
  45.2 0.7 fusion.205
  46.3 0.9 dynamic-slice_bitcast_fusion.5
  48.3 1.1 dynamic-slice_bitcast_fusion.6
  49.4 16.0 %fusion.203 = f32[21,8,64,16]{2,3,1,0:T(8,128)S(1)} fusion(f32[8,64,128]{2,1,0:T(8,128)S(1)} %get-tuple-element.566, f32[8,64,128]{2,1,0:T(8,128)S(1)} %get-tuple-element.567, pred[21]{0:T(512)(128)(4,1)S(1)} %get-tuple-element.568, pred[21]{0:T(512)(128)(4,1)S(1)} %get-tuple-element.569, pred[21]{0:T(512)(128)(4,1)S(1)} %get-tuple-element.570, ...), kind=kOutput, calls=%fused_computation.4.clone.1 | convolution fusion | flops 295895040 | bytes 1384700 | tf_op jit(solution)/shard_map/while/body/eval_jaxpr/jtxy,jky->jtxk/dot_general | solution.py:109
  65.4 1.6 fusion.204
  67.1 0.7 fusion.205
  67.8 0.4 concatenate.36
  68.2 0.9 dynamic-slice_bitcast_fusion.5
  70.2 1.1 dynamic-slice_bitcast_fusion.6
  71.3 16.0 %fusion.203 = f32[21,8,64,16]{2,3,1,0:T(8,128)S(1)} fusion(f32[8,64,128]{2,1,0:T(8,128)S(1)} %get-tuple-element.566, f32[8,64,128]{2,1,0:T(8,128)S(1)} %get-tuple-element.567, pred[21]{0:T(512)(128)(4,1)S(1)} %get-tuple-element.568, pred[21]{0:T(512)(128)(4,1)S(1)} %get-tuple-element.569, pred[21]{0:T(512)(128)(4,1)S(1)} %get-tuple-element.570, ...), kind=kOutput, calls=%fused_computation.4.clone.1 | convolution fusion | flops 295895040 | bytes 1384700 | tf_op jit(solution)/shard_map/while/body/eval_jaxpr/jtxy,jky->jtxk/dot_general | solution.py:109
  87.3 1.6 fusion.204
  88.9 0.7 fusion.205
  89.6 0.4 concatenate.36
  90.0 0.9 dynamic-slice_bitcast_fusion.5
  92.1 1.1 dynamic-slice_bitcast_fusion.6
  93.1 16.0 %fusion.203 = f32[21,8,64,16]{2,3,1,0:T(8,128)S(1)} fusion(f32[8,64,128]{2,1,0:T(8,128)S(1)} %get-tuple-element.566, f32[8,64,128]{2,1,0:T(8,128)S(1)} %get-tuple-element.567, pred[21]{0:T(512)(128)(4,1)S(1)} %get-tuple-element.568, pred[21]{0:T(512)(128)(4,1)S(1)} %get-tuple-element.569, pred[21]{0:T(512)(128)(4,1)S(1)} %get-tuple-element.570, ...), kind=kOutput, calls=%fused_computation.4.clone.1 | convolution fusion | flops 295895040 | bytes 1384700 | tf_op jit(solution)/shard_map/while/body/eval_jaxpr/jtxy,jky->jtxk/dot_general | solution.py:109
  109.1 1.6 fusion.204
  110.8 0.7 fusion.205
  111.5 0.4 concatenate.36
  111.9 0.9 dynamic-slice_bitcast_fusion.5
  113.9 1.1 dynamic-slice_bitcast_fusion.6
  115.0 16.0 %fusion.203 = f32[21,8,64,16]{2,3,1,0:T(8,128)S(1)} fusion(f32[8,64,128]{2,1,0:T(8,128)S(1)} %get-tuple-element.566, f32[8,64,128]{2,1,0:T(8,128)S(1)} %get-tuple-element.567, pred[21]{0:T(512)(128)(4,1)S(1)} %get-tuple-element.568, pred[21]{0:T(512)(128)(4,1)S(1)} %get-tuple-element.569, pred[21]{0:T(512)(128)(4,1)S(1)} %get-tuple-element.570, ...), kind=kOutput, calls=%fused_computation.4.clone.1 | convolution fusion | flops 295895040 | bytes 1384700 | tf_op jit(solution)/shard_map/while/body/eval_jaxpr/jtxy,jky->jtxk/dot_general | solution.py:109
  131.0 1.6 fusion.204
  132.6 0.7 fusion.205
  133.7 0.9 dynamic-slice_bitcast_fusion.5
  135.8 1.1 dynamic-slice_bitcast_fusion.6
  136.9 16.0 %fusion.203 = f32[21,8,64,16]{2,3,1,0:T(8,128)S(1)} fusion(f32[8,64,128]{2,1,0:T(8,128)S(1)} %get-tuple-element.566, f32[8,64,128]{2,1,0:T(8,128)S(1)} %get-tuple-element.567, pred[21]{0:T(512)(128)(4,1)S(1)} %get-tuple-element.568, pred[21]{0:T(512)(128)(4,1)S(1)} %get-tuple-element.569, pred[21]{0:T(512)(128)(4,1)S(1)} %get-tuple-element.570, ...), kind=kOutput, calls=%fused_computation.4.clone.1 | convolution fusion | flops 295895040 | bytes 1384700 | tf_op jit(solution)/shard_map/while/body/eval_jaxpr/jtxy,jky->jtxk/dot_general | solution.py:109
  152.8 1.6 fusion.204
  154.5 0.7 fusion.205
  155.6 0.9 dynamic-slice_bitcast_fusion.5
  157.6 1.1 dynamic-slice_bitcast_fusion.6
  158.7 16.0 %fusion.203 = f32[21,8,64,16]{2,3,1,0:T(8,128)S(1)} fusion(f32[8,64,128]{2,1,0:T(8,128)S(1)} %get-tuple-element.566, f32[8,64,128]{2,1,0:T(8,128)S(1)} %get-tuple-element.567, pred[21]{0:T(512)(128)(4,1)S(1)} %get-tuple-element.568, pred[21]{0:T(512)(128)(4,1)S(1)} %get-tuple-element.569, pred[21]{0:T(512)(128)(4,1)S(1)} %get-tuple-element.570, ...), kind=kOutput, calls=%fused_computation.4.clone.1 | convolution fusion | flops 295895040 | bytes 1384700 | tf_op jit(solution)/shard_map/while/body/eval_jaxpr/jtxy,jky->jtxk/dot_general | solution.py:109
  174.7 1.6 fusion.204
  176.3 0.7 fusion.205
  177.1 0.4 concatenate.36
  177.5 0.9 dynamic-slice_bitcast_fusion.5
  179.6 1.0 copy.33
  180.7 7.0 all-to-all-start
  187.6 20.5 %all-to-all-done = f32[16,23,512]{2,1,0:T(8,128)S(1)} async-done(((f32[16,23,512]{2,1,0:T(8,128)}), f32[16,23,512]{2,1,0:T(8,128)S(1)}, u32[]{:S(2)}, u32[]{:S(2)}) %all-to-all-start) | async-done | bytes 753696 | tf_op jit(solution)/shard_map/all_to_all | solution.py:132
  208.4 3.0 all_gather.3
  211.4 0.7 fusion.167
  212.2 2.8 gather_fusion
  215.0 0.7 multiply_reduce_fusion
  216.5 349.0 %pmax.7 = f32[]{:T(128)} all-reduce(f32[]{:T(128)S(6)} %sqrt.28), channel_id=1, replica_groups=mesh['param'=16,'space'=2,'term'=8] {'param','term'}, use_global_device_ids=true, to_apply=%region_5.6 | all-reduce | flops 1 | bytes 8 | tf_op jit(solution)/shard_map/pmax | solution.py:147
  566.5 342.2 %psum.14 = f32[24]{0:T(128)S(1)} all-reduce(f32[24]{0:T(128)S(1)} %convolution_bitcast_fusion.5), channel_id=1, replica_groups=mesh['param'=16,'space'=2,'term'=8] {'param','term'}, use_global_device_ids=true, to_apply=%region_7.8 | all-reduce | flops 24 | bytes 192 | tf_op jit(solution)/shard_map/psum | solution.py:150
  908.7 0.6 reduce_sum.67
  910.7 344.2 %psum.15 = f32[24]{0:T(128)S(1)} all-reduce(f32[24]{0:T(128)S(1)} %convolution_bitcast_fusion.4), channel_id=1, replica_groups=mesh['param'=16,'space'=2,'term'=8] {'param','term'}, use_global_device_ids=true, to_apply=%region_10.11 | all-reduce | flops 24 | bytes 192 | tf_op jit(solution)/shard_map/psum | solution.py:153
  1254.9 0.6 reduce_sum.69
  1256.5 0.8 fusion.112
  1257.4 0.6 multiply_divide_fusion
  (116 shorter events, 11.5 us)
Async XLA Ops:
  5.7 16.0 %copy-start = (s32[4]{0:T(128)S(1)}, s32[4]{0:T(128)}, u32[]{:S(2)}) copy-start(s32[4]{0:T(128)} %get-tuple-element.619) | copy-start | bytes 52 | tf_op jit(solution)/shard_map/while
  21.7 3.7 copy-start.1
  27.6 16.0 %copy-start = (s32[4]{0:T(128)S(1)}, s32[4]{0:T(128)}, u32[]{:S(2)}) copy-start(s32[4]{0:T(128)} %get-tuple-element.619) | copy-start | bytes 52 | tf_op jit(solution)/shard_map/while
  43.5 3.7 copy-start.1
  49.4 16.0 %copy-start = (s32[4]{0:T(128)S(1)}, s32[4]{0:T(128)}, u32[]{:S(2)}) copy-start(s32[4]{0:T(128)} %get-tuple-element.619) | copy-start | bytes 52 | tf_op jit(solution)/shard_map/while
  65.4 3.7 copy-start.1
  71.3 16.0 %copy-start = (s32[4]{0:T(128)S(1)}, s32[4]{0:T(128)}, u32[]{:S(2)}) copy-start(s32[4]{0:T(128)} %get-tuple-element.619) | copy-start | bytes 52 | tf_op jit(solution)/shard_map/while
  87.2 3.7 copy-start.1
  93.1 16.0 %copy-start = (s32[4]{0:T(128)S(1)}, s32[4]{0:T(128)}, u32[]{:S(2)}) copy-start(s32[4]{0:T(128)} %get-tuple-element.619) | copy-start | bytes 52 | tf_op jit(solution)/shard_map/while
  109.1 3.7 copy-start.1
  115.0 16.0 %copy-start = (s32[4]{0:T(128)S(1)}, s32[4]{0:T(128)}, u32[]{:S(2)}) copy-start(s32[4]{0:T(128)} %get-tuple-element.619) | copy-start | bytes 52 | tf_op jit(solution)/shard_map/while
  131.0 3.7 copy-start.1
  136.8 16.0 %copy-start = (s32[4]{0:T(128)S(1)}, s32[4]{0:T(128)}, u32[]{:S(2)}) copy-start(s32[4]{0:T(128)} %get-tuple-element.619) | copy-start | bytes 52 | tf_op jit(solution)/shard_map/while
  152.8 3.7 copy-start.1
  158.7 16.0 %copy-start = (s32[4]{0:T(128)S(1)}, s32[4]{0:T(128)}, u32[]{:S(2)}) copy-start(s32[4]{0:T(128)} %get-tuple-element.619) | copy-start | bytes 52 | tf_op jit(solution)/shard_map/while
  174.7 3.7 copy-start.1
  180.7 385.7 %copy-start.2 = (s32[168]{0:T(256)S(1)}, s32[168]{0:T(256)}, u32[]{:S(2)}) copy-start(s32[168]{0:T(256)} %param.13) | copy-start | bytes 2020
  180.7 27.5 %all-to-all-start = ((f32[16,23,512]{2,1,0:T(8,128)}), f32[16,23,512]{2,1,0:T(8,128)S(1)}, u32[]{:S(2)}, u32[]{:S(2)}) async-start(f32[16,23,512]{2,1,0:T(8,128)} %bitcast.5), calls=%async_computation | async-start | bytes 1572864 | tf_op jit(solution)/shard_map/all_to_all | solution.py:132
where the time goes:
time: 1260 us
  blocking collectives  1040 us (83%)
  matrix products  157 us (12%)
  local copies, waits for them, and re-layouts  24.8 us (2%)
  waiting for transfers between devices  20.5 us (2%)
    pmax x1, blocking collectives, body(): largest = lax.pmax(jnp.max(frobenius), ('param', 'term'))  349 us
    psum x1, blocking collectives, body(): second_sq = lax.psum(group_squares(second_guess, onehot), ('param', 'term'))  344 us
    psum x1, blocking collectives, body(): first_sq = lax.psum(group_squares(first_guess, onehot), ('param', 'term'))  342 us
    dot_general x8, matrix products, tile_integrals(): across_y = jnp.einsum('jtxy,jky->jtxk', monomial, y_pick, precision=highest)  128 us
  transfers between devices with their start and end apart: 1, of which 1 were waited for; matrix products, arithmetic and copies ran while one was open for 0% of the time, Pallas kernels for 0%

commit v1 on v0

v1 whole, which is shorter than its diff:
```python
import functools

import jax
import jax.numpy as jnp
from jax import lax
from jax.experimental import pallas as pl
from jax.experimental.pallas import tpu as pltpu
from jax.sharding import PartitionSpec as P

NX = 128
NY = 128
NT = 8
POWERS = 7
TERMS = 168
TESTS = 1024
GROUPS = 24
ROWS = 176
WIDE = 256
HALF = 64
GROUP_SIZE = 4
STEPS = 12
EARLY = 4

MESH = pl.DeviceIdType.MESH
f32 = jnp.float32
bf16 = jnp.bfloat16


def iota(shape, dim):
    return lax.broadcasted_iota(jnp.int32, shape, dim)


def split(value):
    high = value.astype(bf16)
    low = (value - high.astype(f32)).astype(bf16)
    return high, low


def bumps(offset):
    scaled = offset.astype(f32) / 16.0
    base = 1.0 - scaled * scaled
    inside = jnp.abs(scaled) < 1.0
    cube = base * base * base
    value = jnp.where(inside, cube * base, 0.0)
    first = jnp.where(inside, 8.0 * scaled * cube / 16.0, 0.0)
    second = jnp.where(inside, -8.0 * (cube - 6.0 * scaled * scaled * base * base) / 256.0, 0.0)
    return value, first, second


def pick_center(which, centers, count):
    total = jnp.zeros_like(which)
    for k in range(count):
        total = jnp.where(which == k, centers[k], total)
    return total


def dot(a, b):
    return jnp.dot(a, b, preferred_element_type=f32)


def dot_nt(a, b):
    return lax.dot_general(a, b, (((1,), (1,)), ((), ())), preferred_element_type=f32)


def kernel(
    n_param,
    n_term,
    fields,
    library,
    centers_x,
    centers_y,
    centers_t,
    groups,
    coefficients,
    misfit,
    pow_u,
    pow_v,
    m_hi,
    m_lo,
    w_hi,
    w_lo,
    bx_hi,
    bx_lo,
    table,
    rows_own,
    rows_far,
    a_hi,
    a_lo,
    corr,
    lib_all,
    code_v,
    code_s,
    msg,
    got_p,
    mid,
    got_t,
    field_sem,
    lib_send,
    lib_recv,
    code_sem,
    row_send,
    row_recv,
    p_send,
    p_recv,
    t_send,
    t_recv,
):
    me_p = lax.axis_index("param")
    me_s = lax.axis_index("space")
    me_t = lax.axis_index("term")
    local_terms = TERMS // n_term

    barrier = pltpu.get_barrier_semaphore()
    pl.semaphore_signal(barrier, inc=1, device_id={"space": 1 - me_s}, device_id_type=MESH)
    for d in range(1, n_param):
        peer = lax.rem(me_p + d, n_param)
        pl.semaphore_signal(barrier, inc=1, device_id={"param": peer}, device_id_type=MESH)
    for d in range(1, n_term):
        peer = lax.rem(me_t + d, n_term)
        pl.semaphore_signal(barrier, inc=1, device_id={"term": peer}, device_id_type=MESH)

    loads = []
    for s, powers in enumerate((pow_u, pow_v)):
        for t in range(NT):
            copy = pltpu.make_async_copy(
                fields.at[me_t, s, t],
                powers.at[1, :, pl.ds(t * NY, NY)],
                field_sem.at[s, t],
            )
            copy.start()
            loads.append(copy)

    lane = iota((NY, WIDE), 1)
    center = pick_center(lane & 15, centers_y, 16)
    offset = ((iota((NY, WIDE), 0) - center + 64) & 127) - 64
    value, first, second = bumps(offset)
    block = lane >> 6
    y_part = jnp.where(block == 1, first, jnp.where(block == 2, second, value))
    lane8 = iota((8, WIDE), 1)
    center_t = pick_center((lane8 >> 4) & 3, centers_t, 4)
    w_sum = jnp.zeros((1, WIDE), f32)
    y_sum = jnp.sum(y_part, axis=0, keepdims=True)
    for t in range(NT):
        scaled = (t - center_t).astype(f32) / 4.0
        base = 1.0 - scaled * scaled
        inside = jnp.abs(scaled) < 1.0
        bump = jnp.where(inside, base * base, 0.0)
        slope = jnp.where(inside, 4.0 * scaled * base / 4.0, 0.0)
        time = jnp.where((lane8 >> 6) == 3, slope, bump)[0:1]
        high, low = split(y_part * time)
        w_hi[pl.ds(t * NY, NY), :] = high
        w_lo[pl.ds(t * NY, NY), :] = low
        w_sum = w_sum + y_sum * time

    row = iota((48, WIDE), 0)
    lane = iota((48, WIDE), 1)
    center = pick_center(row & 15, centers_x, 16)
    offset = (((lane & 63) + me_s * HALF - center + 64) & 127) - 64
    value, first, second = bumps(offset)
    order = row >> 4
    x_part = jnp.where(order == 1, first, jnp.where(order == 2, second, value))
    for i in range(GROUP_SIZE):
        high, low = split(jnp.where((lane >> 6) == i, x_part, 0.0))
        bx_hi[pl.ds(i * 48, 48), :] = high
        bx_lo[pl.ds(i * 48, 48), :] = low

    x_sum = jnp.sum(jnp.where((lane >> 6) == 0, x_part, 0.0), axis=1, keepdims=True)
    for i in range(3):
        constant = x_sum[i * 16 : (i + 1) * 16] * w_sum
        table[2 * i] = constant[:, :NY]
        table[2 * i + 1] = constant[:, NY:]

    for copy in loads:
        copy.wait()
    pow_u[0] = jnp.ones((HALF, NT * NY), f32)
    pow_v[0] = jnp.ones((HALF, NT * NY), f32)
    for degree in range(2, POWERS):
        pow_u[degree] = pow_u[degree - 1] * pow_u[1]
        pow_v[degree] = pow_v[degree - 1] * pow_v[1]

    def group_step(g, carry):
        for i in range(GROUP_SIZE):
            q = g * GROUP_SIZE + (i + 1)
            a = q // POWERS
            b = q - a * POWERS
            high, low = split(pow_u[a] * pow_v[b])
            m_hi[pl.ds(i * HALF, HALF), :] = high
            m_lo[pl.ds(i * HALF, HALF), :] = low
        hi = m_hi[...]
        across = dot(hi, w_hi[...]) + dot(m_lo[...], w_hi[...]) + dot(hi, w_lo[...])
        s_hi, s_lo = split(across)
        out = dot(bx_hi[...], s_hi) + dot(bx_lo[...], s_hi) + dot(bx_hi[...], s_lo)
        for i in range(GROUP_SIZE * 3):
            spot = (g * GROUP_SIZE + 1) * 6 + 2 * i
            table[spot] = out[i * 16 : (i + 1) * 16, :NY]
            table[spot + 1] = out[i * 16 : (i + 1) * 16, NY:]
        return carry

    lax.fori_loop(0, EARLY, group_step, 0)

    pl.semaphore_wait(barrier, n_param + n_term - 1)
    lib_all[me_t] = library[...]
    lib_copies = []
    for d in range(1, n_term):
        peer = lax.rem(me_t + d, n_term)
        copy = pltpu.make_async_remote_copy(
            src_ref=library,
            dst_ref=lib_all.at[me_t],
            send_sem=lib_send.at[d],
            recv_sem=lib_recv.at[me_t],
            device_id={"term": peer},
            device_id_type=MESH,
        )
        copy.start()
        lib_copies.append(copy)

    lax.fori_loop(EARLY, STEPS, group_step, 0)

    for d, copy in enumerate(lib_copies, 1):
        copy.wait_send()
        peer = lax.rem(me_t + d, n_term)
        pltpu.make_async_remote_copy(
            src_ref=library,
            dst_ref=lib_all.at[peer],
            send_sem=lib_send.at[d],
            recv_sem=lib_recv.at[peer],
            device_id={"term": peer},
            device_id_type=MESH,
        ).wait_recv()
    for z in range(n_term):
        part = lib_all[z]
        code = ((part[0:1] * POWERS + part[1:2]) * 3 + part[2:3]) * 4 + part[3:4]
        code_v[z : z + 1, 0:local_terms] = code
    copy = pltpu.make_async_copy(code_v, code_s, code_sem)
    copy.start()
    copy.wait()

    left = iota((8, NY), 1) < 64

    def pick(index, odd):
        both = table[index]
        low, high = both[0:8], both[8:16]
        even_row = jnp.where(left, low, pltpu.roll(high, 64, 1))
        odd_row = jnp.where(left, pltpu.roll(low, 64, 1), high)
        return jnp.where(odd == 1, odd_row, even_row)

    def row_copy(c, count):
        return pltpu.make_async_remote_copy(
            src_ref=rows_own.at[pl.ds(c * local_terms * 8, count * 8), :],
            dst_ref=rows_far.at[pl.ds(c * local_terms * 8, count * 8), :],
            send_sem=row_send.at[c],
            recv_sem=row_recv.at[c],
            device_id={"space": 1 - me_s},
            device_id_type=MESH,
        )

    for s, monomial in enumerate((POWERS, 1)):
        rows_own[pl.ds((TERMS + s) * 8, 8), :] = pick(monomial * 6 + 1, 1)
    rows_own[pl.ds((TERMS + 2) * 8, (ROWS - TERMS - 2) * 8), :] = jnp.zeros(
        ((ROWS - TERMS - 2) * 8, NY), f32
    )

    def pick_step(z, carry):
        for i in range(local_terms):
            code = code_s[z, i]
            spot = pl.multiple_of((z * local_terms + i) * 8, 8)
            rows_own[pl.ds(spot, 8), :] = pick(code >> 1, code & 1)
        return carry

    pick_step(0, 0)
    tail_copy = row_copy(n_term, ROWS - TERMS)
    tail_copy.start()
    for z in range(1, n_term):
        pick_step(z, 0)
        row_copy(z - 1, local_terms).start()
    row_copy(n_term - 1, local_terms).start()

    group_row = groups[...]
    lane_w = iota((ROWS, WIDE), 1)
    row_w = iota((ROWS, WIDE), 0)
    eye = lane_w == row_w
    term_mask = (lane_w < TERMS) & (row_w < TERMS)
    wide_groups = jnp.where(iota((1, WIDE), 1) < TERMS, group_row, -1)
    group_col = jnp.sum(jnp.where(eye, wide_groups, 0), axis=1, keepdims=True)
    group_col = jnp.where(iota((ROWS, 1), 0) < TERMS, group_col, -1)
    onehot = jnp.where(group_col == iota((ROWS, NY), 1), 1.0, 0.0)
    onehot_t = jnp.where(wide_groups == iota((32, WIDE), 0), 1.0, 0.0)
    eye_g = iota((32, NY), 0) == iota((32, NY), 1)

    a_hi[pl.ds(ROWS, WIDE - ROWS), :] = jnp.zeros((WIDE - ROWS, TESTS), bf16)
    a_lo[pl.ds(ROWS, WIDE - ROWS), :] = jnp.zeros((WIDE - ROWS, TESTS), bf16)
    for z in range(n_term):
        row_copy(z, local_terms).wait()
    tail_copy.wait()

    for s in range(8):
        own = rows_own[pl.ds(s, ROWS, stride=8), :]
        far = rows_far[pl.ds(s, ROWS, stride=8), :]
        high, low = split(own + far)
        a_hi[pl.ds(0, ROWS), pl.ds(s * NY, NY)] = high
        a_lo[pl.ds(0, ROWS), pl.ds(s * NY, NY)] = low
    lhs = a_hi[pl.ds(0, ROWS), :]
    gram = (
        dot_nt(lhs, a_hi[...])
        + dot_nt(lhs, a_lo[...])
        + dot_nt(a_lo[pl.ds(0, ROWS), :], a_hi[...])
    )

    diagonal = jnp.where(eye, gram, 0.0)
    scale_row = 1.0 / jnp.sqrt(jnp.sum(diagonal, axis=0, keepdims=True) / TESTS + 1e-06)
    scale_col = 1.0 / jnp.sqrt(jnp.sum(diagonal, axis=1, keepdims=True) / TESTS + 1e-06)
    normal = gram * (scale_col / TESTS) * scale_row
    correlation = jnp.where(term_mask, normal, 0.0)
    corr[...] = correlation
    frobenius_sq = jnp.sum(jnp.sum(correlation * correlation, axis=1, keepdims=True), axis=0, keepdims=True)
    lane_row = iota((1, WIDE), 1)
    right_rows = []
    right_cols = []
    for s in range(2):
        right_rows.append(jnp.where(lane_row < TERMS, normal[TERMS + s : TERMS + s + 1], 0.0))
        column = jnp.sum(jnp.where(lane_w == TERMS + s, normal, 0.0), axis=1, keepdims=True)
        right_cols.append(jnp.where(iota((ROWS, 1), 0) < TERMS, column, 0.0))

    lane_g = iota((1, NY), 1)

    def combine(stack):
        return jnp.where(
            lane_g < GROUPS, jnp.sum(stack, axis=0), jnp.max(stack, axis=0)
        )

    def exchange(use, axis, count, me, source, target, send_sem, recv_sem):
        target[use, me] = source[use]
        copies = []
        for d in range(1, count):
            peer = lax.rem(me + d, count)
            copy = pltpu.make_async_remote_copy(
                src_ref=source.at[use],
                dst_ref=target.at[use, me],
                send_sem=send_sem.at[use, d],
                recv_sem=recv_sem.at[use, me],
                device_id={axis: peer},
                device_id_type=MESH,
            )
            copy.start()
            copies.append(copy)
        for d in range(1, count):
            peer = lax.rem(me + d, count)
            pltpu.make_async_remote_copy(
                src_ref=source.at[use],
                dst_ref=target.at[use, peer],
                send_sem=send_sem.at[use, d],
                recv_sem=recv_sem.at[use, peer],
                device_id={axis: peer},
                device_id_type=MESH,
            ).wait_recv()
        return copies

    def all_reduce(use, message):
        msg[use] = message
        sent = exchange(use, "param", n_param, me_p, msg, got_p, p_send, p_recv)
        mid[use] = combine(got_p[use])
        sent += exchange(use, "term", n_term, me_t, mid, got_t, t_send, t_recv)
        total = combine(got_t[use])
        return total, sent

    def factors(totals):
        valid = jnp.where(lane_g < GROUPS, totals, 0.0)
        mean = jnp.sum(valid, axis=1, keepdims=True) / GROUPS
        threshold = 0.7 * jnp.sqrt(mean)
        factor = jnp.maximum(0.0, 1.0 - threshold / jnp.sqrt(valid + 1e-12))
        factor = jnp.where(lane_g < GROUPS, factor, 0.0)
        col = jnp.sum(onehot * factor, axis=1, keepdims=True)
        group_factor = jnp.sum(jnp.where(eye_g, factor, 0.0), axis=1, keepdims=True)
        row = jnp.sum(onehot_t * group_factor, axis=0, keepdims=True)
        return row, col

    squares = right_cols[0] * right_cols[0] + right_cols[1] * right_cols[1]
    first_sq = jnp.sum(onehot * squares, axis=0, keepdims=True)
    message = jnp.where(lane_g < GROUPS, first_sq, frobenius_sq)
    total, sent_first = all_reduce(0, message)
    largest_sq = jnp.max(jnp.where(lane_g < GROUPS, 0.0, total), axis=1, keepdims=True)
    largest = jnp.sqrt(largest_sq)
    step_size = 1.0 / largest
    factor_row, factor_col = factors(total * (step_size * step_size))
    matrix = corr[...]
    guess_cols = []
    squares = jnp.zeros((ROWS, 1), f32)
    for s in range(2):
        first_row = step_size * right_rows[s] * factor_row
        first_col = step_size * right_cols[s] * factor_col
        product = jnp.sum(matrix * first_row, axis=1, keepdims=True)
        guess = first_col - step_size * (product - right_cols[s])
        squares = squares + guess * guess
        guess_cols.append(guess)
    second_sq = jnp.sum(onehot * squares, axis=0, keepdims=True)
    total, sent_second = all_reduce(1, jnp.where(lane_g < GROUPS, second_sq, 0.0))
    factor_row, factor_col = factors(total)
    for s in range(2):
        guess_row = jnp.sum(jnp.where(eye, guess_cols[s], 0.0), axis=0, keepdims=True)
        coefficient = guess_row * factor_row * largest
        product = jnp.sum(matrix * (guess_cols[s] * factor_col), axis=0, keepdims=True)
        coefficients[0, s : s + 1, :] = coefficient[:, :TERMS]
        misfit[0, s : s + 1, :] = (right_rows[s] - product)[:, :TERMS]
    for copy in sent_first + sent_second:
        copy.wait_send()


def body(fields, library, centers_x, centers_y, centers_t, groups):
    n_param = lax.axis_size("param")
    n_term = lax.axis_size("term")
    local_terms = library.shape[0]
    vmem = pl.BlockSpec(memory_space=pltpu.VMEM)
    smem = pl.BlockSpec(memory_space=pltpu.SMEM)
    out = jax.ShapeDtypeStruct((1, 2, TERMS), f32)
    wide_groups = jnp.pad(groups, (0, WIDE - TERMS)).reshape(1, WIDE)
    dma = pltpu.SemaphoreType.DMA
    return pl.pallas_call(
        functools.partial(kernel, n_param, n_term),
        out_shape=(out, out),
        in_specs=[pl.BlockSpec(memory_space=pl.ANY), vmem, smem, smem, smem, vmem],
        out_specs=(vmem, vmem),
        scratch_shapes=[
            pltpu.VMEM((POWERS, HALF, NT * NY), f32),
            pltpu.VMEM((POWERS, HALF, NT * NY), f32),
            pltpu.VMEM((GROUP_SIZE * HALF, NT * NY), bf16),
            pltpu.VMEM((GROUP_SIZE * HALF, NT * NY), bf16),
            pltpu.VMEM((NT * NY, WIDE), bf16),
            pltpu.VMEM((NT * NY, WIDE), bf16),
            pltpu.VMEM((GROUP_SIZE * 48, WIDE), bf16),
            pltpu.VMEM((GROUP_SIZE * 48, WIDE), bf16),
            pltpu.VMEM((POWERS * POWERS * 6, 16, NY), f32),
            pltpu.VMEM((ROWS * 8, NY), f32),
            pltpu.VMEM((ROWS * 8, NY), f32),
            pltpu.VMEM((WIDE, TESTS), bf16),
            pltpu.VMEM((WIDE, TESTS), bf16),
            pltpu.VMEM((ROWS, WIDE), f32),
            pltpu.VMEM((n_term, 4, local_terms), jnp.int32),
            pltpu.VMEM((8, NY), jnp.int32),
            pltpu.SMEM((8, NY), jnp.int32),
            pltpu.VMEM((2, 1, NY), f32),
            pltpu.VMEM((2, n_param, 1, NY), f32),
            pltpu.VMEM((2, 1, NY), f32),
            pltpu.VMEM((2, n_term, 1, NY), f32),
            dma((2, NT)),
            dma((n_term,)),
            dma((n_term,)),
            dma,
            dma((n_term + 1,)),
            dma((n_term + 1,)),
            dma((2, n_param)),
            dma((2, n_param)),
            dma((2, n_term)),
            dma((2, n_term)),
        ],
        compiler_params=pltpu.CompilerParams(
            collective_id=0, has_side_effects=True, vmem_limit_bytes=48 * 1024 * 1024
        ),
    )(fields, library.T, centers_x, centers_y, centers_t, wide_groups)


def solution(mesh):
    return jax.shard_map(
        body,
        mesh=mesh,
        in_specs=(P("param", None, None, "space", None), P("term", None), P(), P(), P(), P()),
        out_specs=(P(("param", "term"), None, None), P(("param", "term"), None, None)),
        check_vma=False,
    )
```

time: 1260 us -> 48.9 us (0.04)
  the two profiles are of different devices: /device:TPU:0 before, /device:TPU:6 now
where the time goes in v1:
time: 48.9 us; the launch traced here: 48.7 us
  Pallas kernels  41.4 us (85%)
  local copies, waits for them, and re-layouts  6.67 us (14%)
  between operations  0.64 us (1%)
    pallas_call x1, Pallas kernels, body(): pl.pallas_call(functools.partial(kernel, n_param, n_term), out_shape=(out...  41.4 us
    unnamed x12, local copies, waits for them, and re-layouts  5.99 us

profile of v1, /device:TPU:6, one launch (start us, length us, event | category | flops | bytes accessed | tf_op | source)
XLA Modules:
  0.0 48.7 jit_solution(9356669137405991093)
XLA Ops:
  0.6 0.7 %pad.4 = s32[256]{0:T(256)S(1)} pad(s32[168]{0:T(256)} %param.11, s32[]{:T(128)} %constant.0.clone.1), padding=0_88 | pad | bytes 1700 | tf_op jit(solution)/shard_map/jit(_pad)/pad | solution.py:415
  1.3 0.0 copy-start
  1.3 2.2 %copy-done = f32[8,2,8,64,128]{4,3,2,1,0:T(8,128)S(1)} copy-done((f32[8,2,8,64,128]{4,3,2,1,0:T(8,128)S(1)}, f32[8,2,8,64,128]{4,3,2,1,0:T(8,128)}, u32[]{:S(2)}) %copy-start) | copy-done | bytes 4194328
  3.5 0.0 copy-start.1
  3.5 0.7 %copy-done.1 = s32[21,4]{0,1:T(4,128)S(1)} copy-done((s32[21,4]{0,1:T(4,128)S(1)}, s32[21,4]{0,1:T(4,128)}, u32[]{:S(2)}) %copy-start.1) | copy-done | bytes 360
  4.2 0.0 copy-start.2
  4.2 0.7 %copy-done.2 = s32[16]{0:T(128)S(1)} copy-done((s32[16]{0:T(128)S(1)}, s32[16]{0:T(128)}, u32[]{:S(2)}) %copy-start.2) | copy-done | bytes 88
  4.8 0.0 copy-start.3
  4.8 0.7 %copy-done.3 = s32[16]{0:T(128)S(1)} copy-done((s32[16]{0:T(128)S(1)}, s32[16]{0:T(128)}, u32[]{:S(2)}) %copy-start.3) | copy-done | bytes 88
  5.5 0.0 copy-start.4
  5.5 0.7 %copy-done.4 = s32[4]{0:T(128)S(1)} copy-done((s32[4]{0:T(128)S(1)}, s32[4]{0:T(128)}, u32[]{:S(2)}) %copy-start.4) | copy-done | bytes 40
  6.2 41.4 %shard_map.77 = (f32[1,2,168]{2,1,0:T(2,128)S(1)}, f32[1,2,168]{2,1,0:T(2,128)S(1)}) custom-call(f32[8,2,8,64,128]{4,3,2,1,0:T(8,128)S(1)} %copy-done, s32[4,21]{1,0:T(4,128)S(1)} %bitcast.3, s32[16]{0:T(128)S(1)} %copy-done.2, s32[16]{0:T(128)S(1)} %copy-done.3, s32[4]{0:T(128)S(1)} %copy-done.4, s32[1,256]{1,0:T(1,128)S(1)} %bitcast.2), custom_call_target="tpu_custom_call" | custom-call | tf_op jit(solution)/shard_map/pallas_call | solution.py:417
  47.5 0.6 %copy.10 = f32[1,2,168]{2,1,0:T(2,128)} copy(f32[1,2,168]{2,1,0:T(2,128)S(1)} %get-tuple-element.4) | data formatting | bytes 2688
  48.1 0.6 %copy.11 = f32[1,2,168]{2,1,0:T(2,128)} copy(f32[1,2,168]{2,1,0:T(2,128)S(1)} %get-tuple-element.5) | data formatting | bytes 2688
Async XLA Ops:
  1.3 2.2 %copy-start = (f32[8,2,8,64,128]{4,3,2,1,0:T(8,128)S(1)}, f32[8,2,8,64,128]{4,3,2,1,0:T(8,128)}, u32[]{:S(2)}) copy-start(f32[8,2,8,64,128]{4,3,2,1,0:T(8,128)} %fields.1) | copy-start | bytes 12582916
  3.5 0.7 %copy-start.1 = (s32[21,4]{0,1:T(4,128)S(1)}, s32[21,4]{0,1:T(4,128)}, u32[]{:S(2)}) copy-start(s32[21,4]{0,1:T(4,128)} %param.7) | copy-start | bytes 1012
  4.2 0.7 %copy-start.2 = (s32[16]{0:T(128)S(1)}, s32[16]{0:T(128)}, u32[]{:S(2)}) copy-start(s32[16]{0:T(128)} %centers_x.1) | copy-start | bytes 196
  4.8 0.7 %copy-start.3 = (s32[16]{0:T(128)S(1)}, s32[16]{0:T(128)}, u32[]{:S(2)}) copy-start(s32[16]{0:T(128)} %centers_y.1) | copy-start | bytes 196
  5.5 0.7 %copy-start.4 = (s32[4]{0:T(128)S(1)}, s32[4]{0:T(128)}, u32[]{:S(2)}) copy-start(s32[4]{0:T(128)} %centers_t.1) | copy-start | bytes 52

commit v2 on v1

--- a/solution.py
+++ b/solution.py
@@ -66,13 +66,18 @@
     n_param,
     n_term,
     fields,
+    library_in,
+    centers_x_in,
+    centers_y_in,
+    centers_t_in,
+    groups_in,
+    outputs,
     library,
     centers_x,
     centers_y,
     centers_t,
     groups,
-    coefficients,
-    misfit,
+    small_sem,
     pow_u,
     pow_v,
     m_hi,
@@ -119,6 +124,19 @@
         peer = lax.rem(me_t + d, n_term)
         pl.semaphore_signal(barrier, inc=1, device_id={"term": peer}, device_id_type=MESH)
 
+    smalls = []
+    for i, (source, target) in enumerate(
+        (
+            (centers_y_in, centers_y),
+            (centers_t_in, centers_t),
+            (centers_x_in, centers_x),
+            (library_in, library),
+            (groups_in, groups),
+        )
+    ):
+        copy = pltpu.make_async_copy(source, target, small_sem.at[i])
+        copy.start()
+        smalls.append(copy)
     loads = []
     for s, powers in enumerate((pow_u, pow_v)):
         for t in range(NT):
@@ -129,6 +147,9 @@
             )
             copy.start()
             loads.append(copy)
+
+    for copy in smalls:
+        copy.wait()
 
     lane = iota((NY, WIDE), 1)
     center = pick_center(lane & 15, centers_y, 16)
@@ -275,12 +296,13 @@
         row_copy(z - 1, local_terms).start()
     row_copy(n_term - 1, local_terms).start()
 
-    group_row = groups[...]
     lane_w = iota((ROWS, WIDE), 1)
     row_w = iota((ROWS, WIDE), 0)
     eye = lane_w == row_w
     term_mask = (lane_w < TERMS) & (row_w < TERMS)
-    wide_groups = jnp.where(iota((1, WIDE), 1) < TERMS, group_row, -1)
+    wide_groups = jnp.concatenate(
+        [groups[...], jnp.full((1, WIDE - TERMS), -1, jnp.int32)], axis=1
+    )
     group_col = jnp.sum(jnp.where(eye, wide_groups, 0), axis=1, keepdims=True)
     group_col = jnp.where(iota((ROWS, 1), 0) < TERMS, group_col, -1)
     onehot = jnp.where(group_col == iota((ROWS, NY), 1), 1.0, 0.0)
@@ -399,8 +421,8 @@
         guess_row = jnp.sum(jnp.where(eye, guess_cols[s], 0.0), axis=0, keepdims=True)
         coefficient = guess_row * factor_row * largest
         product = jnp.sum(matrix * (guess_cols[s] * factor_col), axis=0, keepdims=True)
-        coefficients[0, s : s + 1, :] = coefficient[:, :TERMS]
-        misfit[0, s : s + 1, :] = (right_rows[s] - product)[:, :TERMS]
+        outputs[0, s : s + 1, :] = coefficient[:, :TERMS]
+        outputs[1, s : s + 1, :] = (right_rows[s] - product)[:, :TERMS]
     for copy in sent_first + sent_second:
         copy.wait_send()
 
@@ -410,16 +432,20 @@
     n_term = lax.axis_size("term")
     local_terms = library.shape[0]
     vmem = pl.BlockSpec(memory_space=pltpu.VMEM)
-    smem = pl.BlockSpec(memory_space=pltpu.SMEM)
-    out = jax.ShapeDtypeStruct((1, 2, TERMS), f32)
-    wide_groups = jnp.pad(groups, (0, WIDE - TERMS)).reshape(1, WIDE)
+    hbm = pl.BlockSpec(memory_space=pltpu.HBM)
     dma = pltpu.SemaphoreType.DMA
-    return pl.pallas_call(
+    outputs = pl.pallas_call(
         functools.partial(kernel, n_param, n_term),
-        out_shape=(out, out),
-        in_specs=[pl.BlockSpec(memory_space=pl.ANY), vmem, smem, smem, smem, vmem],
-        out_specs=(vmem, vmem),
+        out_shape=jax.ShapeDtypeStruct((2, 2, TERMS), f32),
+        in_specs=[hbm] * 6,
+        out_specs=vmem,
         scratch_shapes=[
+            pltpu.VMEM((4, local_terms), jnp.int32),
+            pltpu.SMEM(centers_x.shape, jnp.int32),
+            pltpu.SMEM(centers_y.shape, jnp.int32),
+            pltpu.SMEM(centers_t.shape, jnp.int32),
+            pltpu.VMEM((1, TERMS), jnp.int32),
+            dma((5,)),
             pltpu.VMEM((POWERS, HALF, NT * NY), f32),
             pltpu.VMEM((POWERS, HALF, NT * NY), f32),
             pltpu.VMEM((GROUP_SIZE * HALF, NT * NY), bf16),
@@ -453,9 +479,10 @@
             dma((2, n_term)),
         ],
         compiler_params=pltpu.CompilerParams(
-            collective_id=0, has_side_effects=True, vmem_limit_bytes=48 * 1024 * 1024
+            collective_id=0, has_side_effects=True, vmem_limit_bytes=67043328
         ),
-    )(fields, library.T, centers_x, centers_y, centers_t, wide_groups)
+    )(fields, library.T, centers_x, centers_y, centers_t, groups.reshape(1, TERMS))
+    return outputs[0:1], outputs[1:2]
 
 
 def solution(mesh):

time: 48.9 us -> 44.8 us (0.916)
  local copies, waits for them, and re-layouts: 6.67 us -> 1.26 us
  Pallas kernels: 41.4 us -> 42.8 us
    unnamed x12 -> x0, local copies, waits for them, and re-layouts: 5.99 us -> none
    pallas_call x1, Pallas kernels: 41.4 us -> 42.8 us  [body(): pl.pallas_call(functools.partial(kernel, n_param, n_term), out_shape=jax....]
    slice x0 -> x1, local copies, waits for them, and re-layouts: none -> 1.26 us  [body(): return (outputs[0:1], outputs[1:2])]
    pad x1 -> x0, local copies, waits for them, and re-layouts: 0.68 us -> none  [body(): wide_groups = jnp.pad(groups, (0, WIDE - TERMS)).reshape(1, WIDE)]
where the time goes in v2:
time: 44.8 us; the launch traced here: 44.6 us
  Pallas kernels  42.8 us (96%)
  local copies, waits for them, and re-layouts  1.26 us (3%)
  between operations  0.64 us (1%)
    pallas_call x1, Pallas kernels, body(): pl.pallas_call(functools.partial(kernel, n_param, n_term), out_shape=jax....  42.8 us
    slice x1, local copies, waits for them, and re-layouts, body(): return (outputs[0:1], outputs[1:2])  1.26 us

profile of v2, /device:TPU:6, one launch (start us, length us, event | category | flops | bytes accessed | tf_op | source)
XLA Modules:
  0.0 44.6 jit_solution(10457525709222153181)
XLA Ops:
  0.6 42.8 %shard_map.77 = f32[2,2,168]{2,1,0:T(2,128)} custom-call(f32[8,2,8,64,128]{4,3,2,1,0:T(8,128)} %fields.1, s32[4,21]{1,0:T(4,128)} %bitcast.2, s32[16]{0:T(128)} %centers_x_in.1, s32[16]{0:T(128)} %centers_y_in.1, s32[4]{0:T(128)} %centers_t_in.1, s32[1,168]{1,0:T(1,128)} %bitcast.3), custom_call_target="tpu_custom_call" | custom-call | tf_op jit(solution)/shard_map/pallas_call | solution.py:437
  43.4 1.3 %fusion = (f32[1,2,168]{2,1,0:T(2,128)}, f32[1,2,168]{2,1,0:T(2,128)}) fusion(f32[2,2,168]{2,1,0:T(2,128)} %shard_map.77), kind=kLoop, calls=%fused_computation | loop fusion | bytes 5376 | tf_op jit(solution)/shard_map/slice | solution.py:485

commit v3 on v2

--- a/solution.py
+++ b/solution.py
@@ -80,12 +80,12 @@
     small_sem,
     pow_u,
     pow_v,
-    m_hi,
-    m_lo,
+    blocks,
     w_hi,
     w_lo,
-    bx_hi,
-    bx_lo,
+    bx,
+    held_hi,
+    held_lo,
     table,
     rows_own,
     rows_far,
@@ -182,14 +182,8 @@
     x_part = jnp.where(order == 1, first, jnp.where(order == 2, second, value))
     for i in range(GROUP_SIZE):
         high, low = split(jnp.where((lane >> 6) == i, x_part, 0.0))
-        bx_hi[pl.ds(i * 48, 48), :] = high
-        bx_lo[pl.ds(i * 48, 48), :] = low
-
-    x_sum = jnp.sum(jnp.where((lane >> 6) == 0, x_part, 0.0), axis=1, keepdims=True)
-    for i in range(3):
-        constant = x_sum[i * 16 : (i + 1) * 16] * w_sum
-        table[2 * i] = constant[:, :NY]
-        table[2 * i + 1] = constant[:, NY:]
+        bx[pl.ds(i * 48, 48), :] = high
+        bx[pl.ds((GROUP_SIZE + i) * 48, 48), :] = low
 
     for copy in loads:
         copy.wait()
@@ -199,24 +193,34 @@
         pow_u[degree] = pow_u[degree - 1] * pow_u[1]
         pow_v[degree] = pow_v[degree - 1] * pow_v[1]
 
+    rows, height = GROUP_SIZE * 48, GROUP_SIZE * HALF
+
+    def finish(g):
+        both = dot(bx[...], held_hi[...])
+        out = both[:rows] + both[rows:] + dot(bx[pl.ds(0, rows), :], held_lo[...])
+        for i in range(GROUP_SIZE * 3):
+            spot = (g * GROUP_SIZE + GROUP_SIZE) * 6 + 2 * i
+            table[spot] = out[i * 16 : (i + 1) * 16, :NY]
+            table[spot + 1] = out[i * 16 : (i + 1) * 16, NY:]
+
     def group_step(g, carry):
+        finish(g - 1)
         for i in range(GROUP_SIZE):
             q = g * GROUP_SIZE + (i + 1)
             a = q // POWERS
             b = q - a * POWERS
             high, low = split(pow_u[a] * pow_v[b])
-            m_hi[pl.ds(i * HALF, HALF), :] = high
-            m_lo[pl.ds(i * HALF, HALF), :] = low
-        hi = m_hi[...]
-        across = dot(hi, w_hi[...]) + dot(m_lo[...], w_hi[...]) + dot(hi, w_lo[...])
-        s_hi, s_lo = split(across)
-        out = dot(bx_hi[...], s_hi) + dot(bx_lo[...], s_hi) + dot(bx_hi[...], s_lo)
-        for i in range(GROUP_SIZE * 3):
-            spot = (g * GROUP_SIZE + 1) * 6 + 2 * i
-            table[spot] = out[i * 16 : (i + 1) * 16, :NY]
-            table[spot + 1] = out[i * 16 : (i + 1) * 16, NY:]
+            blocks[pl.ds(i * HALF, HALF), :] = high
+            blocks[pl.ds(height + i * HALF, HALF), :] = low
+        both = dot(blocks[...], w_hi[...])
+        across = both[:height] + both[height:] + dot(blocks[pl.ds(0, height), :], w_lo[...])
+        high, low = split(across)
+        held_hi[...] = high
+        held_lo[...] = low
         return carry
 
+    held_hi[...] = jnp.zeros((height, WIDE), bf16)
+    held_lo[...] = jnp.zeros((height, WIDE), bf16)
     lax.fori_loop(0, EARLY, group_step, 0)
 
     pl.semaphore_wait(barrier, n_param + n_term - 1)
@@ -236,6 +240,13 @@
         lib_copies.append(copy)
 
     lax.fori_loop(EARLY, STEPS, group_step, 0)
+    finish(STEPS - 1)
+
+    x_sum = jnp.sum(jnp.where((lane >> 6) == 0, x_part, 0.0), axis=1, keepdims=True)
+    for i in range(3):
+        constant = x_sum[i * 16 : (i + 1) * 16] * w_sum
+        table[18 + 2 * i] = constant[:, :NY]
+        table[18 + 2 * i + 1] = constant[:, NY:]
 
     for d, copy in enumerate(lib_copies, 1):
         copy.wait_send()
@@ -276,7 +287,7 @@
         )
 
     for s, monomial in enumerate((POWERS, 1)):
-        rows_own[pl.ds((TERMS + s) * 8, 8), :] = pick(monomial * 6 + 1, 1)
+        rows_own[pl.ds((TERMS + s) * 8, 8), :] = pick(monomial * 6 + 19, 1)
     rows_own[pl.ds((TERMS + 2) * 8, (ROWS - TERMS - 2) * 8), :] = jnp.zeros(
         ((ROWS - TERMS - 2) * 8, NY), f32
     )
@@ -285,7 +296,7 @@
         for i in range(local_terms):
             code = code_s[z, i]
             spot = pl.multiple_of((z * local_terms + i) * 8, 8)
-            rows_own[pl.ds(spot, 8), :] = pick(code >> 1, code & 1)
+            rows_own[pl.ds(spot, 8), :] = pick((code >> 1) + 18, code & 1)
         return carry
 
     pick_step(0, 0)
@@ -448,13 +459,13 @@
             dma((5,)),
             pltpu.VMEM((POWERS, HALF, NT * NY), f32),
             pltpu.VMEM((POWERS, HALF, NT * NY), f32),
-            pltpu.VMEM((GROUP_SIZE * HALF, NT * NY), bf16),
-            pltpu.VMEM((GROUP_SIZE * HALF, NT * NY), bf16),
+            pltpu.VMEM((2 * GROUP_SIZE * HALF, NT * NY), bf16),
             pltpu.VMEM((NT * NY, WIDE), bf16),
             pltpu.VMEM((NT * NY, WIDE), bf16),
-            pltpu.VMEM((GROUP_SIZE * 48, WIDE), bf16),
-            pltpu.VMEM((GROUP_SIZE * 48, WIDE), bf16),
-            pltpu.VMEM((POWERS * POWERS * 6, 16, NY), f32),
+            pltpu.VMEM((2 * GROUP_SIZE * 48, WIDE), bf16),
+            pltpu.VMEM((GROUP_SIZE * HALF, WIDE), bf16),
+            pltpu.VMEM((GROUP_SIZE * HALF, WIDE), bf16),
+            pltpu.VMEM(((POWERS * POWERS + 3) * 6, 16, NY), f32),
             pltpu.VMEM((ROWS * 8, NY), f32),
             pltpu.VMEM((ROWS * 8, NY), f32),
             pltpu.VMEM((WIDE, TESTS), bf16),

time: 44.8 us -> 41.7 us (0.931)
  Pallas kernels: 42.8 us -> 39.6 us
    pallas_call x1, Pallas kernels: 42.8 us -> 39.6 us  [body(): pl.pallas_call(functools.partial(kernel, n_param, n_term), out_shape=jax....]
where the time goes in v3:
time: 41.7 us; the launch traced here: 41.5 us
  Pallas kernels  39.6 us (95%)
  local copies, waits for them, and re-layouts  1.26 us (3%)
  between operations  0.64 us (2%)
    pallas_call x1, Pallas kernels, body(): pl.pallas_call(functools.partial(kernel, n_param, n_term), out_shape=jax....  39.6 us
    slice x1, local copies, waits for them, and re-layouts, body(): return (outputs[0:1], outputs[1:2])  1.26 us

profile of v3, /device:TPU:6, one launch (start us, length us, event | category | flops | bytes accessed | tf_op | source)
XLA Modules:
  0.0 41.5 jit_solution(8296563104419401861)
XLA Ops:
  0.6 39.6 %shard_map.77 = f32[2,2,168]{2,1,0:T(2,128)} custom-call(f32[8,2,8,64,128]{4,3,2,1,0:T(8,128)} %fields.1, s32[4,21]{1,0:T(4,128)} %bitcast.2, s32[16]{0:T(128)} %centers_x_in.1, s32[16]{0:T(128)} %centers_y_in.1, s32[4]{0:T(128)} %centers_t_in.1, s32[1,168]{1,0:T(1,128)} %bitcast.3), custom_call_target="tpu_custom_call" | custom-call | tf_op jit(solution)/shard_map/pallas_call | solution.py:448
  40.3 1.3 %fusion = (f32[1,2,168]{2,1,0:T(2,128)}, f32[1,2,168]{2,1,0:T(2,128)}) fusion(f32[2,2,168]{2,1,0:T(2,128)} %shard_map.77), kind=kLoop, calls=%fused_computation | loop fusion | bytes 5376 | tf_op jit(solution)/shard_map/slice | solution.py:496

commit v4 on v3

--- a/solution.py
+++ b/solution.py
@@ -20,6 +20,7 @@
 GROUP_SIZE = 4
 STEPS = 12
 EARLY = 4
+CHUNK = 128
 
 MESH = pl.DeviceIdType.MESH
 f32 = jnp.float32
@@ -195,13 +196,19 @@
 
     rows, height = GROUP_SIZE * 48, GROUP_SIZE * HALF
 
+    left = iota((8, NY), 1) < 64
+
+    def spread(spot, block):
+        for i in range(2):
+            low, high = block[0:8, i * NY : (i + 1) * NY], block[8:16, i * NY : (i + 1) * NY]
+            table[spot + 2 * i] = jnp.where(left, low, pltpu.roll(high, 64, 1))
+            table[spot + 2 * i + 1] = jnp.where(left, pltpu.roll(low, 64, 1), high)
+
     def finish(g):
         both = dot(bx[...], held_hi[...])
         out = both[:rows] + both[rows:] + dot(bx[pl.ds(0, rows), :], held_lo[...])
         for i in range(GROUP_SIZE * 3):
-            spot = (g * GROUP_SIZE + GROUP_SIZE) * 6 + 2 * i
-            table[spot] = out[i * 16 : (i + 1) * 16, :NY]
-            table[spot + 1] = out[i * 16 : (i + 1) * 16, NY:]
+            spread((g * GROUP_SIZE + GROUP_SIZE) * 12 + 4 * i, out[i * 16 : (i + 1) * 16])
 
     def group_step(g, carry):
         finish(g - 1)
@@ -209,9 +216,11 @@
             q = g * GROUP_SIZE + (i + 1)
             a = q // POWERS
             b = q - a * POWERS
-            high, low = split(pow_u[a] * pow_v[b])
-            blocks[pl.ds(i * HALF, HALF), :] = high
-            blocks[pl.ds(height + i * HALF, HALF), :] = low
+            for k in range(NT * NY // CHUNK):
+                columns = pl.ds(k * CHUNK, CHUNK)
+                high, low = split(pow_u[a, :, columns] * pow_v[b, :, columns])
+                blocks[pl.ds(i * HALF, HALF), columns] = high
+                blocks[pl.ds(height + i * HALF, HALF), columns] = low
         both = dot(blocks[...], w_hi[...])
         across = both[:height] + both[height:] + dot(blocks[pl.ds(0, height), :], w_lo[...])
         high, low = split(across)
@@ -245,8 +254,7 @@
     x_sum = jnp.sum(jnp.where((lane >> 6) == 0, x_part, 0.0), axis=1, keepdims=True)
     for i in range(3):
         constant = x_sum[i * 16 : (i + 1) * 16] * w_sum
-        table[18 + 2 * i] = constant[:, :NY]
-        table[18 + 2 * i + 1] = constant[:, NY:]
+        spread(36 + 4 * i, constant)
 
     for d, copy in enumerate(lib_copies, 1):
         copy.wait_send()
@@ -267,15 +275,6 @@
     copy.start()
     copy.wait()
 
-    left = iota((8, NY), 1) < 64
-
-    def pick(index, odd):
-        both = table[index]
-        low, high = both[0:8], both[8:16]
-        even_row = jnp.where(left, low, pltpu.roll(high, 64, 1))
-        odd_row = jnp.where(left, pltpu.roll(low, 64, 1), high)
-        return jnp.where(odd == 1, odd_row, even_row)
-
     def row_copy(c, count):
         return pltpu.make_async_remote_copy(
             src_ref=rows_own.at[pl.ds(c * local_terms * 8, count * 8), :],
@@ -287,7 +286,7 @@
         )
 
     for s, monomial in enumerate((POWERS, 1)):
-        rows_own[pl.ds((TERMS + s) * 8, 8), :] = pick(monomial * 6 + 19, 1)
+        rows_own[pl.ds((TERMS + s) * 8, 8), :] = table[monomial * 12 + 39]
     rows_own[pl.ds((TERMS + 2) * 8, (ROWS - TERMS - 2) * 8), :] = jnp.zeros(
         ((ROWS - TERMS - 2) * 8, NY), f32
     )
@@ -296,7 +295,7 @@
         for i in range(local_terms):
             code = code_s[z, i]
             spot = pl.multiple_of((z * local_terms + i) * 8, 8)
-            rows_own[pl.ds(spot, 8), :] = pick((code >> 1) + 18, code & 1)
+            rows_own[pl.ds(spot, 8), :] = table[code + 36]
         return carry
 
     pick_step(0, 0)
@@ -465,7 +464,7 @@
             pltpu.VMEM((2 * GROUP_SIZE * 48, WIDE), bf16),
             pltpu.VMEM((GROUP_SIZE * HALF, WIDE), bf16),
             pltpu.VMEM((GROUP_SIZE * HALF, WIDE), bf16),
-            pltpu.VMEM(((POWERS * POWERS + 3) * 6, 16, NY), f32),
+            pltpu.VMEM(((POWERS * POWERS + 3) * 12, 8, NY), f32),
             pltpu.VMEM((ROWS * 8, NY), f32),
             pltpu.VMEM((ROWS * 8, NY), f32),
             pltpu.VMEM((WIDE, TESTS), bf16),

time: 41.7 us -> 41.4 us (level)
  no operation moved by 1% of the time
where the time goes in v4:
time: 41.4 us; the launch traced here: 41.2 us
  Pallas kernels  39.3 us (95%)
  local copies, waits for them, and re-layouts  1.26 us (3%)
  between operations  0.64 us (2%)
    pallas_call x1, Pallas kernels, body(): pl.pallas_call(functools.partial(kernel, n_param, n_term), out_shape=jax....  39.3 us
    slice x1, local copies, waits for them, and re-layouts, body(): return (outputs[0:1], outputs[1:2])  1.26 us

profile of v4, /device:TPU:6, one launch (start us, length us, event | category | flops | bytes accessed | tf_op | source)
XLA Modules:
  0.0 41.2 jit_solution(17707761978440054211)
XLA Ops:
  0.6 39.3 %shard_map.77 = f32[2,2,168]{2,1,0:T(2,128)} custom-call(f32[8,2,8,64,128]{4,3,2,1,0:T(8,128)} %fields.1, s32[4,21]{1,0:T(4,128)} %bitcast.2, s32[16]{0:T(128)} %centers_x_in.1, s32[16]{0:T(128)} %centers_y_in.1, s32[4]{0:T(128)} %centers_t_in.1, s32[1,168]{1,0:T(1,128)} %bitcast.3), custom_call_target="tpu_custom_call" | custom-call | tf_op jit(solution)/shard_map/pallas_call | solution.py:447
  40.0 1.3 %fusion = (f32[1,2,168]{2,1,0:T(2,128)}, f32[1,2,168]{2,1,0:T(2,128)}) fusion(f32[2,2,168]{2,1,0:T(2,128)} %shard_map.77), kind=kLoop, calls=%fused_computation | loop fusion | bytes 5376 | tf_op jit(solution)/shard_map/slice | solution.py:495

commit v5 on v4

--- a/solution.py
+++ b/solution.py
@@ -153,7 +153,7 @@
         copy.wait()
 
     lane = iota((NY, WIDE), 1)
-    center = pick_center(lane & 15, centers_y, 16)
+    center = pick_center(iota((8, WIDE), 1) & 15, centers_y, 16)[0:1]
     offset = ((iota((NY, WIDE), 0) - center + 64) & 127) - 64
     value, first, second = bumps(offset)
     block = lane >> 6
@@ -176,7 +176,7 @@
 
     row = iota((48, WIDE), 0)
     lane = iota((48, WIDE), 1)
-    center = pick_center(row & 15, centers_x, 16)
+    center = pick_center(iota((48, NY), 0) & 15, centers_x, 16)[:, 0:1]
     offset = (((lane & 63) + me_s * HALF - center + 64) & 127) - 64
     value, first, second = bumps(offset)
     order = row >> 4
@@ -186,13 +186,18 @@
         bx[pl.ds(i * 48, 48), :] = high
         bx[pl.ds((GROUP_SIZE + i) * 48, 48), :] = low
 
+    pow_u[0] = jnp.ones((HALF, NT * NY), f32)
+    pow_v[0] = jnp.ones((HALF, NT * NY), f32)
     for copy in loads:
         copy.wait()
-    pow_u[0] = jnp.ones((HALF, NT * NY), f32)
-    pow_v[0] = jnp.ones((HALF, NT * NY), f32)
-    for degree in range(2, POWERS):
-        pow_u[degree] = pow_u[degree - 1] * pow_u[1]
-        pow_v[degree] = pow_v[degree - 1] * pow_v[1]
+    for powers in (pow_u, pow_v):
+        for k in range(NT * NY // CHUNK):
+            columns = pl.ds(k * CHUNK, CHUNK)
+            base = powers[1, :, columns]
+            product = base
+            for degree in range(2, POWERS):
+                product = product * base
+                powers[degree, :, columns] = product
 
     rows, height = GROUP_SIZE * 48, GROUP_SIZE * HALF
 

time: 41.4 us -> 41.4 us (level)
  no operation moved by 1% of the time
where the time goes in v5:
time: 41.4 us; the launch traced here: 41.2 us
  Pallas kernels  39.3 us (95%)
  local copies, waits for them, and re-layouts  1.26 us (3%)
  between operations  0.64 us (2%)
    pallas_call x1, Pallas kernels, body(): pl.pallas_call(functools.partial(kernel, n_param, n_term), out_shape=jax....  39.3 us
    slice x1, local copies, waits for them, and re-layouts, body(): return (outputs[0:1], outputs[1:2])  1.26 us

profile of v5, /device:TPU:6, one launch (start us, length us, event | category | flops | bytes accessed | tf_op | source)
XLA Modules:
  0.0 41.2 jit_solution(1519507912472458898)
XLA Ops:
  0.6 39.3 %shard_map.77 = f32[2,2,168]{2,1,0:T(2,128)} custom-call(f32[8,2,8,64,128]{4,3,2,1,0:T(8,128)} %fields.1, s32[4,21]{1,0:T(4,128)} %bitcast.2, s32[16]{0:T(128)} %centers_x_in.1, s32[16]{0:T(128)} %centers_y_in.1, s32[4]{0:T(128)} %centers_t_in.1, s32[1,168]{1,0:T(1,128)} %bitcast.3), custom_call_target="tpu_custom_call" | custom-call | tf_op jit(solution)/shard_map/pallas_call | solution.py:452
  40.0 1.3 %fusion = (f32[1,2,168]{2,1,0:T(2,128)}, f32[1,2,168]{2,1,0:T(2,128)}) fusion(f32[2,2,168]{2,1,0:T(2,128)} %shard_map.77), kind=kLoop, calls=%fused_computation | loop fusion | bytes 5376 | tf_op jit(solution)/shard_map/slice | solution.py:500
